TPU v7x, 256 devices: a whole 4x4x8 slice. The times are simulated.
256 devices in a mesh: pole: 4 (over y), row: 8 (over z_lo, x), col: 8 (over z_hi, core).
Axes of the slice: x: 4, y: 4, z: 8 (z_hi: 4, z_lo: 2; z = z_hi * 2 + z_lo), core: 2. Of those that a mesh axis runs over, the one named last changes fastest.
Arguments:
- found_inverse: bfloat16 [4, 2, 8192, 8, 8, 128], P('pole', None, 'row', None, 'col'), may hold values from -0.125 to 0.125
- l_panel: bfloat16 [4, 2, 8192, 512], P('pole', None, ('row', 'col')), may hold values from -1.5 to 1.5
- block_pattern: int32 [64, 4], P(('row', 'col')), may hold values 0 or 1
- sup_widths: int32 [4], replicated, may hold values from 1 to 128, 320 in all
- diag_inverse: bfloat16 [4, 2, 512, 128], P('pole'), may hold values from -6 to 6
- pole_weights: float32 [4, 2], P('pole'), may hold values from -4 to 4
Outputs:
- density: float32 [512, 8192], P('col', 'row')
- diagonal: float32 [512, 128], replicated
Inputs may be any that keep to these rules, and one draw needn't show every extreme that they name: `sup_widths`: one supernode has exactly 128 columns.
All inputs are finite; a program needn't handle non-finite values. No bound on the sum of `block_pattern` on one device may be relied on, other than what follows from the above.
Results may differ from a plain program's by a relative error of at most 0.0003.
Values may be sent and summed in bfloat16 or wider, within the bound.
A program may use at most 128 MiB of HBM per device.

v0:
```python
import jax
import jax.numpy as jnp
from jax import lax
from jax.sharding import PartitionSpec as P


def contract(left, right):
    return jnp.einsum("jk,ij->ki", left, right, preferred_element_type=jnp.float32)


def pair_product(left, right):
    return jnp.einsum("ika,kbi->kab", left, right, precision=lax.Precision.HIGHEST)


def per_device(found_inverse, l_panel, block_pattern, sup_widths, diag_inverse, pole_weights):
    slot_width = diag_inverse.shape[-1]
    total_cols = l_panel.shape[-1]
    supernodes = total_cols // slot_width
    row_count = lax.axis_size("row")
    row_index = lax.axis_index("row")
    col_index = lax.axis_index("col")
    columns = jnp.arange(total_cols, dtype=jnp.int32)
    column_ok = columns % slot_width < jnp.repeat(sup_widths, slot_width)
    block_ok = jnp.repeat(block_pattern[0], slot_width) == 1
    masked = jnp.where(
        (column_ok & block_ok)[None, None, :], l_panel[0], jnp.zeros((), jnp.bfloat16)
    )
    column_rows = lax.all_gather(masked, "row", axis=1, tiled=True)
    own_rows = lax.all_gather(masked, "col", axis=1, tiled=True)
    local_rows = found_inverse.shape[2]
    inverse = found_inverse[0].reshape(2, local_rows, row_count * slot_width)
    part_real = contract(column_rows[1], inverse[1]) - contract(column_rows[0], inverse[0])
    part_imag = -(contract(column_rows[1], inverse[0]) + contract(column_rows[0], inverse[1]))
    w_real = pole_weights[0, 0]
    w_imag = pole_weights[0, 1]
    weighted = w_real * part_real - w_imag * part_imag
    part = lax.psum_scatter(weighted, "col", scatter_dimension=0, tiled=True)
    density = lax.psum(part, "pole")
    lifted = own_rows.astype(jnp.float32).reshape(2, local_rows, supernodes, slot_width)
    upper_real = part_real.reshape(supernodes, slot_width, local_rows)
    upper_imag = part_imag.reshape(supernodes, slot_width, local_rows)
    t_real = pair_product(lifted[0], upper_real) - pair_product(lifted[1], upper_imag)
    t_imag = pair_product(lifted[0], upper_imag) + pair_product(lifted[1], upper_real)
    lead_flag = ((row_index == 0) & (col_index == 0)).astype(jnp.float32)
    d_real = diag_inverse[0, 0].astype(jnp.float32).reshape(supernodes, slot_width, slot_width)
    d_imag = diag_inverse[0, 1].astype(jnp.float32).reshape(supernodes, slot_width, slot_width)
    local_term = lead_flag * (w_real * d_real - w_imag * d_imag) - (
        w_real * t_real - w_imag * t_imag
    )
    diagonal = lax.psum(local_term.reshape(total_cols, slot_width), ("pole", "row", "col"))
    return (density, diagonal)


def solution(mesh):
    in_specs = (
        P("pole", None, "row", None, "col", None),
        P("pole", None, ("row", "col"), None),
        P(("row", "col"), None),
        P(),
        P("pole", None, None, None),
        P("pole", None),
    )
    out_specs = (P("col", "row"), P())
    return jax.shard_map(
        per_device, mesh=mesh, in_specs=in_specs, out_specs=out_specs, check_vma=False
    )
```

profile of v0, /device:TPU:2, one launch (start us, length us, event | category | flops | bytes accessed | tf_op | source)
XLA Modules:
  0.0 457.6 jit_solution(11535285280863356408)
XLA Ops:
  7.9 0.7 fusion.25
  8.6 1.7 bitcast_select_fusion
  11.1 1.4 fusion.28
  12.5 3.8 fusion.26
  16.3 38.6 %all-gather.3.cloned.1.call-done = bf16[2,1024,512]{2,1,0:T(8,128)(2,1)} async-done(((bf16[2,128,512]{2,1,0:T(8,128)(2,1)}), bf16[2,1024,512]{2,1,0:T(8,128)(2,1)}) %all-gather.3.cloned.1.call-update) | async-done | bytes 2097168 | tf_op jit(solution)/shard_map/all_gather | solution.py:28
  54.9 2.7 fusion.2
  57.6 1.3 fusion
  59.2 1.3 fusion.12
  60.5 4.6 %multiply_subtract_fusion = (f32[512,1024]{1,0:T(8,128)}, f32[512,1024]{1,0:T(8,128)}) fusion(f32[512,1024]{1,0:T(8,128)S(1)} %fusion.12, f32[]{:T(128)} %bitcast.7, f32[]{:T(128)} %bitcast, f32[512,1024]{1,0:T(8,128)S(1)} %fusion, bf16[128,8,8,128]{3,2,1,0:T(8,128)(2,1)S(1)} %bitcast.67, bf16[2,1024,512]{2,1,0:T(8,128)(2,1)S(1)} %copy-done.3), kind=kOutput, calls=%fused_computation.8 | convolution fusion | flops 1076363264 | bytes 11534344 | tf_op jit(solution)/shard_map/jk,ij->ki/dot_general | solution.py:8
  65.2 0.9 copy-done.4
  66.1 1.3 subtract_multiply_fusion
  67.4 27.9 %all-gather.5.cloned.1.call-done = bf16[2,1024,512]{2,1,0:T(8,128)(2,1)} async-done(((bf16[2,128,512]{2,1,0:T(8,128)(2,1)}), bf16[2,1024,512]{2,1,0:T(8,128)(2,1)}) %all-gather.5.cloned.1.call-update) | async-done | bytes 2097168 | tf_op jit(solution)/shard_map/all_gather | solution.py:29
  95.3 2.7 fusion.27
  97.9 1.3 copy.8
  99.3 1.5 copy.9
  100.8 2.5 fusion.29
  103.3 1.2 fusion.30
  104.5 1.9 fusion.20
  106.4 2.5 fusion.19
  109.0 31.0 %reduce-scatter.2.cloned.1.call-done = f32[64,1024]{1,0:T(8,128)} async-done(((f32[512,1024]{1,0:T(8,128)}), f32[64,1024]{1,0:T(8,128)}) %reduce-scatter.2.cloned.1.call-update) | async-done | bytes 262160 | tf_op jit(solution)/shard_map/reduce_scatter | solution.py:37
  140.1 259.7 %all-reduce.5.cloned.1.call-done = f32[512,128]{1,0:T(8,128)} async-done(((f32[512,128]{1,0:T(8,128)}), f32[512,128]{1,0:T(8,128)}) %all-reduce.5.cloned.1.call-update) | async-done | bytes 262160 | tf_op jit(solution)/shard_map/psum | solution.py:50
  399.8 48.0 %all-reduce.3.cloned.1.call-done = f32[64,1024]{1,0:T(8,128)} async-done(((f32[64,1024]{1,0:T(8,128)}), f32[64,1024]{1,0:T(8,128)}) %all-reduce.3.cloned.1.call-update) | async-done | bytes 262160 | tf_op jit(solution)/shard_map/psum | solution.py:38
  447.8 1.7 copy.36
  449.4 1.7 copy.37
  (20 shorter events, 1.9 us)
Async XLA Ops:
  7.2 47.7 %all-gather.3.cloned.1.call-start = ((), (), s32[]{:S(2)}) async-start(), calls=%async_computation.1 | async-start | bytes 2359296 | tf_op jit(solution)/shard_map/all_gather | solution.py:28
  10.3 85.0 %all-gather.5.cloned.1.call-start = ((), (), s32[]{:S(2)}) async-start(), calls=%async_computation.4 | async-start | bytes 2359296 | tf_op jit(solution)/shard_map/all_gather | solution.py:29
  11.1 129.0 %reduce-scatter.2.cloned.1.call-start = ((), (), s32[]{:S(2)}) async-start(), calls=%async_computation.2 | async-start | bytes 2359296 | tf_op jit(solution)/shard_map/reduce_scatter | solution.py:37
  54.9 2.7 copy-start.3
  57.6 1.6 copy-start.2
  65.1 0.9 copy-start.4
  65.1 334.7 %all-reduce.5.cloned.1.call-start = ((), (), s32[]{:S(2)}) async-start(), calls=%async_computation.5 | async-start | bytes 524288 | tf_op jit(solution)/shard_map/psum | solution.py:50
  100.8 2.6 copy-start
  100.8 2.6 copy-start.1
  108.9 338.8 %all-reduce.3.cloned.1.call-start = ((), (), s32[]{:S(2)}) async-start(), calls=%async_computation.3 | async-start | bytes 524288 | tf_op jit(solution)/shard_map/psum | solution.py:38
Sparse Core Ops, SparseCore 0:
  10.4 44.4 all-gather.2
  57.3 37.9 all-gather.4
  97.8 42.1 reduce-scatter.1
  145.9 253.8 all-reduce.4
  402.0 45.7 all-reduce.2
where the time goes:
time: 458 us
  waiting for transfers between devices  406 us (89%)
  matrix products  18 us (4%)
  local copies, waits for them, and re-layouts  15.2 us (3%)
  between operations  13.9 us (3%)
    psum x1, waiting for transfers between devices, per_device(): lax.psum(local_term.reshape(total_cols, slot_width), ('pole', 'row', 'col'))  260 us
    psum x1, waiting for transfers between devices, per_device(): density = lax.psum(part, 'pole')  48 us
    all_gather x1, waiting for transfers between devices, per_device(): column_rows = lax.all_gather(masked, 'row', axis=1, tiled=True)  38.6 us
    reduce_scatter x1, waiting for transfers between devices, per_device(): part = lax.psum_scatter(weighted, 'col', scatter_dimension=0, tiled=True)  31 us
    all_gather x1, waiting for transfers between devices, per_device(): own_rows = lax.all_gather(masked, 'col', axis=1, tiled=True)  27.9 us
    dot_general x4, matrix products, contract(): jnp.einsum('jk,ij->ki', left, right, preferred_element_type=jnp.float32)  9.92 us
  transfers between devices with their start and end apart: 5, of which 5 were waited for; matrix products, arithmetic and copies ran while one was open for 7% of the time, Pallas kernels for 0%

commit v1 on v0

--- a/solution.py
+++ b/solution.py
@@ -47,7 +47,9 @@
     local_term = lead_flag * (w_real * d_real - w_imag * d_imag) - (
         w_real * t_real - w_imag * t_imag
     )
-    diagonal = lax.psum(local_term.reshape(total_cols, slot_width), ("pole", "row", "col"))
+    diagonal = lax.psum(
+        lax.psum(local_term.reshape(total_cols, slot_width), "pole"), ("row", "col")
+    )
     return (density, diagonal)
 
 

time: 458 us -> 384 us (0.84)
  waiting for transfers between devices: 406 us -> 330 us
    psum x1, waiting for transfers between devices: 260 us -> 180 us  [per_device(): lax.psum(lax.psum(local_term.reshape(total_cols, slot_width), 'pole'), ('...]
  transfers between devices with their start and end apart: 5 -> 5, of which waited for: 5 -> 5; matrix products, arithmetic and copies ran while one was open for 7% -> 8% of each run, Pallas kernels for 0% -> 0%
where the time goes in v1:
time: 384 us; the launch traced here: 381 us
  waiting for transfers between devices  330 us (86%)
  matrix products  17.9 us (5%)
  local copies, waits for them, and re-layouts  15.1 us (4%)
  between operations  13.9 us (4%)
  other arithmetic  4.31 us (1%)
    psum x1, waiting for transfers between devices, per_device(): lax.psum(lax.psum(local_term.reshape(total_cols, slot_width), 'pole'), ('...  180 us
    psum x1, waiting for transfers between devices, per_device(): density = lax.psum(part, 'pole')  50.8 us
    all_gather x1, waiting for transfers between devices, per_device(): column_rows = lax.all_gather(masked, 'row', axis=1, tiled=True)  38.6 us
    reduce_scatter x1, waiting for transfers between devices, per_device(): part = lax.psum_scatter(weighted, 'col', scatter_dimension=0, tiled=True)  31.2 us
    all_gather x1, waiting for transfers between devices, per_device(): own_rows = lax.all_gather(masked, 'col', axis=1, tiled=True)  27.9 us
    dot_general x4, matrix products, contract(): jnp.einsum('jk,ij->ki', left, right, preferred_element_type=jnp.float32)  9.92 us
    dot_general x4, matrix products, pair_product(): jnp.einsum('ika,kbi->kab', left, right, precision=lax.Precision.HIGHEST)  8.03 us
  transfers between devices with their start and end apart: 5, of which 5 were waited for; matrix products, arithmetic and copies ran while one was open for 8% of the time, Pallas kernels for 0%

profile of v1, /device:TPU:2, one launch (start us, length us, event | category | flops | bytes accessed | tf_op | source)
XLA Modules:
  0.0 381.0 jit_solution(16032095371703476693)
XLA Ops:
  7.9 0.7 fusion.25
  8.6 1.7 bitcast_select_fusion
  11.1 1.3 fusion.28
  12.4 3.8 %fusion.26 = (bf16[1,1,1024,8,1,128]{5,3,4,2,1,0:T(8,128)(2,1)}, bf16[1,1,1024,8,1,128]{5,3,4,2,1,0:T(8,128)(2,1)S(1)}) fusion(bf16[1,2,1024,8,1,128]{5,3,4,2,1,0:T(8,128)(2,1)} %param.6), kind=kLoop, calls=%fused_computation.33 | loop fusion | bytes 8388608 | tf_op jit(solution)/shard_map/slice | solution.py:32
  16.2 38.6 %all-gather.3.cloned.1.call-done = bf16[2,1024,512]{2,1,0:T(8,128)(2,1)} async-done(((bf16[2,128,512]{2,1,0:T(8,128)(2,1)}), bf16[2,1024,512]{2,1,0:T(8,128)(2,1)}) %all-gather.3.cloned.1.call-update) | async-done | bytes 2097168 | tf_op jit(solution)/shard_map/all_gather | solution.py:28
  54.9 2.7 fusion.2
  57.6 1.3 fusion
  59.2 1.3 fusion.12
  60.5 4.6 %multiply_subtract_fusion = (f32[512,1024]{1,0:T(8,128)}, f32[512,1024]{1,0:T(8,128)}) fusion(f32[512,1024]{1,0:T(8,128)S(1)} %fusion.12, f32[]{:T(128)} %bitcast.7, f32[]{:T(128)} %bitcast, f32[512,1024]{1,0:T(8,128)S(1)} %fusion, bf16[128,8,8,128]{3,2,1,0:T(8,128)(2,1)S(1)} %bitcast.67, bf16[2,1024,512]{2,1,0:T(8,128)(2,1)S(1)} %copy-done.3), kind=kOutput, calls=%fused_computation.8 | convolution fusion | flops 1076363264 | bytes 11534344 | tf_op jit(solution)/shard_map/jk,ij->ki/dot_general | solution.py:8
  65.2 0.9 copy-done.4
  66.1 1.2 subtract_multiply_fusion
  67.3 27.9 %all-gather.5.cloned.1.call-done = bf16[2,1024,512]{2,1,0:T(8,128)(2,1)} async-done(((bf16[2,128,512]{2,1,0:T(8,128)(2,1)}), bf16[2,1024,512]{2,1,0:T(8,128)(2,1)}) %all-gather.5.cloned.1.call-update) | async-done | bytes 2097168 | tf_op jit(solution)/shard_map/all_gather | solution.py:29
  95.2 2.7 fusion.27
  97.9 1.3 copy.8
  99.2 1.5 copy.9
  100.7 2.5 fusion.29
  103.3 1.2 fusion.30
  104.5 1.9 fusion.20
  106.4 2.4 fusion.19
  108.8 31.2 %reduce-scatter.2.cloned.1.call-done = f32[64,1024]{1,0:T(8,128)} async-done(((f32[512,1024]{1,0:T(8,128)}), f32[64,1024]{1,0:T(8,128)}) %reduce-scatter.2.cloned.1.call-update) | async-done | bytes 262160 | tf_op jit(solution)/shard_map/reduce_scatter | solution.py:37
  140.0 50.8 %all-reduce.6.cloned.1.call-done = (f32[64,1024]{1,0:T(8,128)}, f32[512,128]{1,0:T(8,128)}) async-done(((f32[64,1024]{1,0:T(8,128)}, f32[512,128]{1,0:T(8,128)}), (f32[64,1024]{1,0:T(8,128)}, f32[512,128]{1,0:T(8,128)})) %all-reduce.6.cloned.1.call-update) | async-done | bytes 524304 | tf_op jit(solution)/shard_map/psum | solution.py:38
  190.9 180.2 %all-reduce.4.cloned.1.call-done = f32[512,128]{1,0:T(8,128)} async-done(((f32[512,128]{1,0:T(8,128)}), f32[512,128]{1,0:T(8,128)}) %all-reduce.4.cloned.1.call-update) | async-done | bytes 262160 | tf_op jit(solution)/shard_map/psum | solution.py:50
  371.1 1.7 copy.37
  372.8 1.7 copy.38
  (20 shorter events, 1.9 us)
Async XLA Ops:
  7.2 47.7 %all-gather.3.cloned.1.call-start = ((), (), s32[]{:S(2)}) async-start(), calls=%async_computation.1 | async-start | bytes 2359296 | tf_op jit(solution)/shard_map/all_gather | solution.py:28
  10.3 84.9 %all-gather.5.cloned.1.call-start = ((), (), s32[]{:S(2)}) async-start(), calls=%async_computation.3 | async-start | bytes 2359296 | tf_op jit(solution)/shard_map/all_gather | solution.py:29
  11.1 128.9 %reduce-scatter.2.cloned.1.call-start = ((), (), s32[]{:S(2)}) async-start(), calls=%async_computation.2 | async-start | bytes 2359296 | tf_op jit(solution)/shard_map/reduce_scatter | solution.py:37
  54.9 2.7 copy-start.3
  57.6 1.6 copy-start.2
  65.1 0.9 copy-start.4
  65.1 125.8 %all-reduce.6.cloned.1.call-start = ((), (), s32[]{:S(2)}) async-start(), calls=%async_computation.5 | async-start | bytes 1048576 | tf_op jit(solution)/shard_map/psum | solution.py:38
  100.7 2.6 copy-start
  100.7 2.6 copy-start.1
  140.0 231.1 %all-reduce.4.cloned.1.call-start = ((), (), s32[]{:S(2)}) async-start(), calls=%async_computation.4 | async-start | bytes 524288 | tf_op jit(solution)/shard_map/psum | solution.py:50
Sparse Core Ops, SparseCore 0:
  10.4 44.4 all-gather.2
  57.3 37.9 all-gather.4
  97.8 42.1 reduce-scatter.1
  142.8 48.0 all-reduce.5
  194.2 176.8 all-reduce.3
